TPU v7x, 128 devices: a whole 4x4x4 slice. The times are simulated.
128 devices in a mesh: grp: 8 (over y, core), dom: 16 (over z, x).
Axes of the slice: x: 4, y: 4, z: 4, core: 2. Of those that a mesh axis runs over, the one named last changes fastest.
Arguments:
- diag_blocks: bfloat16 [2048, 384, 384], P(('grp', 'dom')), may hold values from -0.3125 to 0.3125
- face_in: bfloat16 [4096, 384, 384], P(('grp', 'dom')), may hold values from -0.3125 to 0.3125
- face_cross: bfloat16 [2048, 384, 384], P(('grp', 'dom')), may hold values from -0.3125 to 0.3125
- metric: float32 [2048, 384], P(('grp', 'dom')), may hold values from 0.5 to 2
- source_in: int32 [4096], P(('grp', 'dom')), may hold values from 0 to 15
- source_cross: int32 [2048], P(('grp', 'dom')), may hold values from 0 to 15
- orient_in: int32 [4096], P(('grp', 'dom')), may hold values from 0 to 7
- orient_cross: int32 [2048], P(('grp', 'dom')), may hold values from 0 to 7
- peer_in: int32 [4096, 1], P(('grp', 'dom')), may hold values from 0 to 15; in each aligned block of 32 rows (0 to 31, 32 to 63, ...) at most 3 rows name the same one
- peer_cross: int32 [2048, 1], P(('grp', 'dom')), may hold values from 0 to 7; in each aligned block of 16 rows (0 to 15, 16 to 31, ...) at most 3 rows name the same one
- target_in: int32 [4096], P(('grp', 'dom')), may hold values from 0 to 47
- target_cross: int32 [2048], P(('grp', 'dom')), may hold values from 0 to 47
Outputs:
- coarse_diag: float32 [2048, 2304], P('grp')
- coarse_face: float32 [2048, 6912], P('grp')
Inputs may be any that keep to these rules, and one draw needn't show every extreme that they name: `peer_in`: at most 3 records of one device name the same partition; on some device exactly 3 do. `peer_cross`: at most 3 records of one device name the same group; on some device exactly 3 do.
All inputs are finite; a program needn't handle non-finite values.
Results may differ from a plain program's by a relative error of at most 0.0052.
Values may be sent and summed in bfloat16 or wider, within the bound.
A program may use at most 128 MiB of HBM per device.

v0:
```python
import jax
import jax.numpy as jnp
from jax import lax
from jax.sharding import PartitionSpec as P


def corner_table(var_count):
    nodes = -1.0 + 2.0 * jnp.arange(4, dtype=jnp.float32) / 3.0
    basis = jnp.stack(((1.0 - nodes) / 2.0, (1.0 + nodes) / 2.0), axis=1)
    cube = jnp.einsum("ia,jb,kc->abcijk", basis, basis, basis).reshape(8, 64)
    return jnp.kron(jnp.eye(var_count, dtype=jnp.float32), cube)


def restrictor(weights, orient):
    var_count = weights.shape[1] // 64
    table = corner_table(var_count)
    full = weights[:, None, :] * table[None]
    shaped = full.reshape(weights.shape[0], var_count * 8, var_count, 4, 4, 4)
    bits = orient.reshape(-1, 1, 1, 1, 1, 1)
    shaped = jnp.where(bits % 2 == 1, jnp.flip(shaped, 3), shaped)
    shaped = jnp.where(bits // 2 % 2 == 1, jnp.flip(shaped, 4), shaped)
    shaped = jnp.where(bits // 4 % 2 == 1, jnp.flip(shaped, 5), shaped)
    return shaped.reshape(weights.shape[0], var_count * 8, var_count * 64).astype(jnp.bfloat16)


def pick_rows(index, table):
    picks = (index[:, None] == jnp.arange(table.shape[0], dtype=jnp.int32)[None, :]).astype(
        jnp.float32
    )
    return jnp.dot(picks, table, precision=lax.Precision.HIGHEST)


def place_rows(targets, values, row_count):
    picks = (jnp.arange(row_count, dtype=jnp.int32)[:, None] == targets[None, :]).astype(
        jnp.float32
    )
    return jnp.dot(picks, values, precision=lax.Precision.HIGHEST)


def one_sided(blocks, column_side):
    return jnp.einsum(
        "rcj,rij->rci", column_side, blocks, preferred_element_type=jnp.float32
    ).astype(jnp.bfloat16)


def coarse_terms(row_side, products):
    return jnp.einsum("rci,rdi->rcd", row_side, products, preferred_element_type=jnp.float32)


def pack_records(products, targets, peers, peer_count, capacity):
    count = products.shape[0]
    onehot = (peers[:, None] == jnp.arange(peer_count, dtype=jnp.int32)[None, :]).astype(jnp.int32)
    order_rank = jnp.sum((jnp.cumsum(onehot, axis=0) - 1) * onehot, axis=1)
    position = peers * capacity + order_rank
    places = jnp.arange(peer_count * capacity, dtype=jnp.int32)
    picks = places[:, None] == position[None, :]
    flattened = products.reshape(count, -1)
    packed = jnp.dot(
        picks.astype(jnp.bfloat16), flattened, preferred_element_type=jnp.float32
    ).astype(jnp.bfloat16)
    slot_ids = jnp.sum(jnp.where(picks, targets[None, :] + 1, 0), axis=1) - 1
    return (
        packed.reshape((peer_count, capacity) + products.shape[1:]),
        slot_ids.reshape(peer_count, capacity),
    )


def per_device(
    diag_blocks,
    face_in,
    face_cross,
    metric,
    source_in,
    source_cross,
    orient_in,
    orient_cross,
    peer_in,
    peer_cross,
    target_in,
    target_cross,
):
    elem_count = metric.shape[0]
    coarse_width = metric.shape[1] // 8
    square = coarse_width * coarse_width
    group_width = lax.axis_size("dom")
    group_count = lax.axis_size("grp")
    cross_capacity = (face_cross.shape[0] + group_count - 1) // group_count + 1
    inner_capacity = (face_in.shape[0] + group_width - 1) // group_width + 1

    def receive(packet):
        products, slot_ids = packet
        peers_here, items = slot_ids.shape
        flat_ids = slot_ids.reshape(-1)
        row_side = restrictor(
            pick_rows(flat_ids // 3, metric), jnp.zeros(flat_ids.shape, jnp.int32)
        )
        terms = coarse_terms(
            row_side, products.reshape(peers_here * items, products.shape[2], products.shape[3])
        )
        return (terms.reshape(peers_here, items, square), slot_ids)

    diag_side = restrictor(metric, jnp.zeros((elem_count,), jnp.int32))
    diag_coarse = coarse_terms(diag_side, one_sided(diag_blocks, diag_side)).reshape(
        elem_count, square
    )
    cross_side = restrictor(pick_rows(source_cross, metric), orient_cross)
    cross_products = one_sided(face_cross, cross_side)
    inner_side = restrictor(pick_rows(source_in, metric), orient_in)
    inner_products = one_sided(face_in, inner_side)
    cross_packed, cross_ids = pack_records(
        cross_products, target_cross, peer_cross[:, 0], group_count, cross_capacity
    )
    cross_terms, cross_got = receive(
        (
            lax.all_to_all(cross_packed, "grp", split_axis=0, concat_axis=0, tiled=True),
            lax.all_to_all(cross_ids, "grp", split_axis=0, concat_axis=0, tiled=True),
        )
    )
    inner_packed, inner_ids = pack_records(
        inner_products, target_in, peer_in[:, 0], group_width, inner_capacity
    )
    inner_terms, inner_got = receive(
        (
            lax.all_to_all(inner_packed, "dom", split_axis=0, concat_axis=0, tiled=True),
            lax.all_to_all(inner_ids, "dom", split_axis=0, concat_axis=0, tiled=True),
        )
    )
    face_local = place_rows(cross_got.reshape(-1), cross_terms.reshape(-1, square), 3 * elem_count)
    face_local = face_local + place_rows(
        inner_got.reshape(-1), inner_terms.reshape(-1, square), 3 * elem_count
    )
    face_local = face_local.reshape(elem_count, 3 * square)
    coarse_diag, coarse_face = (
        lax.all_gather(diag_coarse, "dom", axis=0, tiled=True),
        lax.all_gather(face_local, "dom", axis=0, tiled=True),
    )
    return (coarse_diag, coarse_face)


def solution(mesh):
    placed = (
        P(("grp", "dom"), None, None),
        P(("grp", "dom"), None, None),
        P(("grp", "dom"), None, None),
        P(("grp", "dom"), None),
        P(("grp", "dom")),
        P(("grp", "dom")),
        P(("grp", "dom")),
        P(("grp", "dom")),
        P(("grp", "dom"), None),
        P(("grp", "dom"), None),
        P(("grp", "dom")),
        P(("grp", "dom")),
    )
    return jax.shard_map(
        per_device,
        mesh=mesh,
        in_specs=placed,
        out_specs=(P("grp", None), P("grp", None)),
        check_vma=False,
    )
```

profile of v0, /device:TPU:1, one launch (start us, length us, event | category | flops | bytes accessed | tf_op | source)
XLA Modules:
  0.0 180.3 jit_solution(1263921991991287014)
XLA Ops:
  7.2 0.7 fusion.33
  7.9 0.8 select_reduce_fusion.3
  8.8 0.7 multiply_add_fusion.1
  9.4 0.1 select_reduce_fusion.2
  9.5 0.7 sub.80
  10.2 6.0 %all-to-all-start = ((s32[8,1,3]{2,1,0:T(1,128)}), s32[8,1,3]{2,1,0:T(1,128)S(1)}, u32[]{:S(2)}, u32[]{:S(2)}) async-start(s32[8,1,3]{2,1,0:T(1,128)} %bitcast.3), calls=%async_computation | async-start | bytes 8192 | tf_op jit(solution)/shard_map/all_to_all | solution.py:116
  16.2 0.1 broadcast_multiply_fusion.3
  16.3 0.1 multiply_bitcast_fusion
  16.4 0.1 mul.177
  16.5 0.1 copy.39
  16.6 0.1 mul.179
  16.7 0.1 mul.174
  16.8 0.1 mul.175
  16.9 0.1 copy.40
  17.0 4.3 %fusion.15 = f32[16,48,48]{2,1,0:T(8,128)S(1)} fusion(bf16[16,384,384]{2,1,0:T(8,128)(2,1)} %param.12, f32[48,384]{1,0:T(8,128)S(1)} %copy.40, f32[16,384]{1,0:T(8,128)} %param.15), kind=kOutput, calls=%fused_computation.25 | convolution fusion | flops 256278528 | bytes 4964352 | tf_op jit(solution)/shard_map/rci,rdi->rcd/dot_general | solution.py:47
  21.4 0.8 reshape.407
  22.3 0.4 fusion.34
  22.6 1.0 broadcast_multiply_fusion.1
  23.7 0.6 reverse_select_fusion.5
  24.3 0.7 reverse_select_fusion.4
  25.0 0.8 fusion.1
  25.8 0.1 slice-done.1
  25.9 1.8 fusion.12
  27.6 0.9 copy.51
  28.6 0.4 fusion.26
  29.0 1.9 %broadcast_multiply_fusion = bf16[32,48,6,4,4,4]{1,0,5,4,3,2:T(8,128)(2,1)S(1)} fusion(f32[48,6,4,4,4]{0,4,3,2,1:T(4,128)S(1)} %broadcast_multiply_fusion.2, f32[32,6,4,4,4]{0,4,3,2,1:T(4,128)S(1)} %bitcast.55), kind=kLoop, calls=%fused_computation.14 | loop fusion | flops 1179648 | bytes 1302528 | tf_op jit(solution)/shard_map/mul | solution.py:17
  31.0 0.1 fusion.25
  31.1 0.1 reduce_window_sum.23
  31.1 0.2 select_reduce_fusion.1
  31.3 1.0 reverse_select_fusion.2
  32.4 0.1 select_reduce_fusion
  32.5 1.5 reverse_select_fusion.1
  34.0 1.1 fusion
  35.1 0.7 sub.86
  35.8 7.6 %all-to-all-start.2 = ((s32[16,1,3]{2,1,0:T(1,128)}), s32[16,1,3]{2,1,0:T(1,128)S(1)}, u32[]{:S(2)}, u32[]{:S(2)}) async-start(s32[16,1,3]{2,1,0:T(1,128)} %bitcast.8), calls=%async_computation.2 | async-start | bytes 16384 | tf_op jit(solution)/shard_map/all_to_all | solution.py:125
  43.4 1.6 convolution_convert_fusion.1
  45.0 1.0 copy.52
  46.0 3.8 %all-to-all-done.2 = s32[16,1,3]{2,1,0:T(1,128)S(1)} async-done(((s32[16,1,3]{2,1,0:T(1,128)}), s32[16,1,3]{2,1,0:T(1,128)S(1)}, u32[]{:S(2)}, u32[]{:S(2)}) %all-to-all-start.2) | async-done | bytes 224 | tf_op jit(solution)/shard_map/all_to_all | solution.py:125
  49.9 6.1 %all-to-all-start.1 = ((bf16[8,3,48,384]{3,2,1,0:T(8,128)(2,1)}), bf16[8,3,48,384]{3,2,1,0:T(8,128)(2,1)}, u32[]{:S(2)}, u32[]{:S(2)}) async-start(bf16[8,3,48,384]{3,2,1,0:T(8,128)(2,1)} %bitcast.49), calls=%async_computation.1 | async-start | bytes 1769472 | tf_op jit(solution)/shard_map/all_to_all | solution.py:115
  55.9 7.7 %fusion.9 = bf16[32,48,384]{2,1,0:T(8,128)(2,1)S(1)} fusion(bf16[32,384,384]{2,1,0:T(8,128)(2,1)} %param.13, bf16[32,48,384]{1,0,2:T(8,128)(2,1)S(1)} %bitcast.42), kind=kOutput, calls=%fused_computation.22 | convolution fusion | flops 453574656 | bytes 11796480 | tf_op jit(solution)/shard_map/rcj,rij->rci/dot_general | solution.py:41
  63.7 0.3 copy.53
  63.9 0.7 convolution_convert_fusion
  64.7 1.4 copy.54
  66.1 3.1 %all-to-all-done.1 = bf16[8,3,48,384]{3,2,1,0:T(8,128)(2,1)} async-done(((bf16[8,3,48,384]{3,2,1,0:T(8,128)(2,1)}), bf16[8,3,48,384]{3,2,1,0:T(8,128)(2,1)}, u32[]{:S(2)}, u32[]{:S(2)}) %all-to-all-start.1) | async-done | bytes 884768 | tf_op jit(solution)/shard_map/all_to_all | solution.py:115
  69.3 3.7 %all-to-all-start.3 = ((bf16[16,3,48,384]{3,2,1,0:T(8,128)(2,1)}), bf16[16,3,48,384]{3,2,1,0:T(8,128)(2,1)S(1)}, u32[]{:S(2)}, u32[]{:S(2)}) async-start(bf16[16,3,48,384]{3,2,1,0:T(8,128)(2,1)} %bitcast.23), calls=%async_computation.3 | async-start | bytes 3538944 | tf_op jit(solution)/shard_map/all_to_all | solution.py:124
  73.0 0.0 all-gather.5.cloned.1.call-start
  73.0 0.5 broadcast.910
  73.5 0.7 reduce.6
  74.2 0.1 eq.232
  74.3 0.2 fusion.30
  74.5 0.7 reduce.7
  75.2 0.1 eq.251
  75.3 0.2 fusion.24
  75.5 1.6 fusion.16
  77.1 0.3 reshape_reshape.6
  77.4 0.3 fusion.23
  77.7 21.1 %all-to-all-done.3 = bf16[16,3,48,384]{3,2,1,0:T(8,128)(2,1)S(1)} async-done(((bf16[16,3,48,384]{3,2,1,0:T(8,128)(2,1)}), bf16[16,3,48,384]{3,2,1,0:T(8,128)(2,1)S(1)}, u32[]{:S(2)}, u32[]{:S(2)}) %all-to-all-start.3) | async-done | bytes 1769504 | tf_op jit(solution)/shard_map/all_to_all | solution.py:124
  98.9 0.7 fusion.4
  99.6 0.5 reshape_reshape.7
  100.2 0.3 convolution_add_fusion
  100.5 0.9 reshape.414
  101.4 62.3 %all-gather.5.cloned.1.call-done = f32[256,6912]{1,0:T(8,128)} async-done(((f32[16,6912]{1,0:T(8,128)}), f32[256,6912]{1,0:T(8,128)}) %all-gather.5.cloned.1.call-update) | async-done | bytes 7077904 | tf_op jit(solution)/shard_map/all_gather | solution.py:135
  163.8 3.2 %copy.65 = f32[256,2304]{1,0:T(8,128)} copy(f32[256,2304]{1,0:T(8,128)} %all-gather.3.cloned.1.call-done) | data formatting | bytes 4718592
  167.0 6.4 %copy.66 = f32[256,6912]{1,0:T(8,128)} copy(f32[256,6912]{1,0:T(8,128)} %all-gather.5.cloned.1.call-done) | data formatting | bytes 14155776
  (36 shorter events, 0.3 us)
Async XLA Ops:
  10.2 25.6 %all-to-all-start = ((s32[8,1,3]{2,1,0:T(1,128)}), s32[8,1,3]{2,1,0:T(1,128)S(1)}, u32[]{:S(2)}, u32[]{:S(2)}) async-start(s32[8,1,3]{2,1,0:T(1,128)} %bitcast.3), calls=%async_computation | async-start | bytes 8192 | tf_op jit(solution)/shard_map/all_to_all | solution.py:116
  16.2 85.3 %all-gather.3.cloned.1.call-start = ((), (), s32[]{:S(2)}) async-start(), calls=%async_computation.4 | async-start | bytes 2506752 | tf_op jit(solution)/shard_map/all_gather | solution.py:134
  17.0 5.2 %copy-start = (f32[16,384]{1,0:T(8,128)S(1)}, f32[16,384]{1,0:T(8,128)}, u32[]{:S(2)}) copy-start(f32[16,384]{1,0:T(8,128)} %param.15) | copy-start | bytes 73732
  17.0 5.2 %copy-start.2 = (s32[16]{0:T(128)S(1)}, s32[16]{0:T(128)}, u32[]{:S(2)}) copy-start(s32[16]{0:T(128)} %param.17) | copy-start | bytes 196
  17.0 8.7 %slice-start = ((s8[4718592]{0:T(1024)(128)(4,1)}), s8[524288]{0:T(1024)(128)(4,1)S(1)}, s32[]{:S(2)}) async-start(s8[4718592]{0:T(1024)(128)(4,1)} %bitcast.46), calls=%async_computation.6 | async-start | bytes 1048576
  21.4 2.3 %copy-start.5 = (s32[16]{0:T(128)S(1)}, s32[16]{0:T(128)}, u32[]{:S(2)}) copy-start(s32[16]{0:T(128)} %param.19) | copy-start | bytes 196
  23.7 2.2 %slice-start.1 = ((s8[4718592]{0:T(1024)(128)(4,1)}), s8[4194304]{0:T(1024)(128)(4,1)S(1)}, s32[]{:S(2)}) async-start(s8[4718592]{0:T(1024)(128)(4,1)} %bitcast.46), calls=%async_computation.7 | async-start | bytes 8388608
  25.9 2.7 %copy-start.3 = (s32[32]{0:T(128)S(1)}, s32[32]{0:T(128)}, u32[]{:S(2)}) copy-start(s32[32]{0:T(128)} %param.16) | copy-start | bytes 388
  29.0 2.0 %copy-start.6 = (s32[32]{0:T(128)S(1)}, s32[32]{0:T(128)}, u32[]{:S(2)}) copy-start(s32[32]{0:T(128)} %param.18) | copy-start | bytes 388
  29.0 2.0 %copy-start.1 = (s32[32,1]{0,1:T(1,128)S(1)}, s32[32,1]{0,1:T(1,128)}, u32[]{:S(2)}) copy-start(s32[32,1]{0,1:T(1,128)} %param.20) | copy-start | bytes 388
  31.3 1.1 copy-start.4
  35.8 14.0 %all-to-all-start.2 = ((s32[16,1,3]{2,1,0:T(1,128)}), s32[16,1,3]{2,1,0:T(1,128)S(1)}, u32[]{:S(2)}, u32[]{:S(2)}) async-start(s32[16,1,3]{2,1,0:T(1,128)} %bitcast.8), calls=%async_computation.2 | async-start | bytes 16384 | tf_op jit(solution)/shard_map/all_to_all | solution.py:125
  49.9 19.4 %all-to-all-start.1 = ((bf16[8,3,48,384]{3,2,1,0:T(8,128)(2,1)}), bf16[8,3,48,384]{3,2,1,0:T(8,128)(2,1)}, u32[]{:S(2)}, u32[]{:S(2)}) async-start(bf16[8,3,48,384]{3,2,1,0:T(8,128)(2,1)} %bitcast.49), calls=%async_computation.1 | async-start | bytes 1769472 | tf_op jit(solution)/shard_map/all_to_all | solution.py:115
  69.3 29.6 %all-to-all-start.3 = ((bf16[16,3,48,384]{3,2,1,0:T(8,128)(2,1)}), bf16[16,3,48,384]{3,2,1,0:T(8,128)(2,1)S(1)}, u32[]{:S(2)}, u32[]{:S(2)}) async-start(bf16[16,3,48,384]{3,2,1,0:T(8,128)(2,1)} %bitcast.23), calls=%async_computation.3 | async-start | bytes 3538944 | tf_op jit(solution)/shard_map/all_to_all | solution.py:124
  73.0 90.8 %all-gather.5.cloned.1.call-start = ((), (), s32[]{:S(2)}) async-start(), calls=%async_computation.5 | async-start | bytes 7520256 | tf_op jit(solution)/shard_map/all_gather | solution.py:135
Sparse Core Ops, SparseCore 0:
  22.4 46.2 all-gather.2
  101.5 62.1 all-gather.4
where the time goes:
time: 181 us; the launch traced here: 180 us
  waiting for transfers between devices  90.5 us (50%)
  starting transfers between devices  23.4 us (13%)
  matrix products  20.3 us (11%)
  local copies, waits for them, and re-layouts  18.6 us (10%)
  between operations  14.4 us (8%)
  other arithmetic  13.1 us (7%)
    all_gather x1, waiting for transfers between devices, per_device(): lax.all_gather(face_local, 'dom', axis=0, tiled=True)  62.3 us
    all_to_all x1, waiting for transfers between devices, per_device(): lax.all_to_all(inner_packed, 'dom', split_axis=0, concat_axis=0, tiled=True)  21.1 us
    unnamed x24, local copies, waits for them, and re-layouts  13.4 us
    dot_general x2, matrix products, one_sided(): jnp.einsum('rcj,rij->rci', column_side, blocks, preferred_element_type=jn...  9.53 us
    all_to_all x1, starting transfers between devices, per_device(): lax.all_to_all(inner_ids, 'dom', split_axis=0, concat_axis=0, tiled=True)  7.6 us
    dot_general x3, matrix products, coarse_terms(): jnp.einsum('rci,rdi->rcd', row_side, products, preferred_element_type=jnp...  6.65 us
    all_to_all x1, starting transfers between devices, per_device(): lax.all_to_all(cross_packed, 'grp', split_axis=0, concat_axis=0, tiled=True)  6.07 us
    all_to_all x1, starting transfers between devices, per_device(): lax.all_to_all(cross_ids, 'grp', split_axis=0, concat_axis=0, tiled=True)  5.96 us
  transfers between devices with their start and end apart: 6, of which 4 were waited for; matrix products, arithmetic and copies ran while one was open for 22% of the time, Pallas kernels for 0%

commit v1 on v0

--- a/solution.py
+++ b/solution.py
@@ -2,6 +2,29 @@
 import jax.numpy as jnp
 from jax import lax
 from jax.sharding import PartitionSpec as P
+
+
+def cut_along(value, dim, size):
+    shape = value.shape
+    blocks = value.reshape(*shape[:dim], size, shape[dim] // size, *shape[dim + 1 :])
+    return jnp.moveaxis(blocks, dim, 0)
+
+
+def in_order(tiles, dim):
+    shape = list(tiles.shape[1:])
+    shape[dim] *= tiles.shape[0]
+    return jnp.moveaxis(tiles, 0, dim).reshape(shape)
+
+
+def swapped_with_each(value, axis, split_dim, concat_dim):
+    size, mine = (lax.axis_size(axis), lax.axis_index(axis))
+    blocks = cut_along(value, split_dim, size)
+    gathered = [blocks[mine]]
+    for step in range(1, size):
+        sent = blocks[mine ^ step]
+        gathered.append(lax.ppermute(sent, axis, [(i, i ^ step) for i in range(size)]))
+    blocks = jnp.stack(gathered)[mine ^ jnp.arange(size)]
+    return in_order(blocks, concat_dim)
 
 
 def corner_table(var_count):
@@ -113,7 +136,7 @@
     cross_terms, cross_got = receive(
         (
             lax.all_to_all(cross_packed, "grp", split_axis=0, concat_axis=0, tiled=True),
-            lax.all_to_all(cross_ids, "grp", split_axis=0, concat_axis=0, tiled=True),
+            swapped_with_each(cross_ids, "grp", 0, 0),
         )
     )
     inner_packed, inner_ids = pack_records(

time: 181 us -> 179 us (0.989)
  waiting for transfers between devices: 90.5 us -> 79.9 us
  starting transfers between devices: 23.4 us -> 30.2 us
  local copies, waits for them, and re-layouts: 18.6 us -> 20.8 us
    all_to_all x1, waiting for transfers between devices: 21.1 us -> 8.92 us  [per_device(): lax.all_to_all(inner_packed, 'dom', split_axis=0, concat_axis=0, tiled=True)]
    ppermute x0 -> x7, starting transfers between devices: none -> 9.34 us  [swapped_with_each(): lax.ppermute(sent, axis, [(i, i ^ step) for i in range(size)])]
    all_to_all x1 -> x0, starting transfers between devices: 5.96 us -> none  [per_device(): lax.all_to_all(cross_ids, 'grp', split_axis=0, concat_axis=0, tiled=True)]
    all_to_all x1, waiting for transfers between devices: 3.84 us -> 0.01 us  [per_device(): lax.all_to_all(inner_ids, 'dom', split_axis=0, concat_axis=0, tiled=True)]
    all_gather x1, waiting for transfers between devices: 62.3 us -> 65.8 us  [per_device(): lax.all_gather(face_local, 'dom', axis=0, tiled=True)]
    all_to_all x1, starting transfers between devices: 3.71 us -> 6.93 us  [per_device(): lax.all_to_all(inner_packed, 'dom', split_axis=0, concat_axis=0, tiled=True)]
    ppermute x0 -> x7, waiting for transfers between devices: none -> 1.99 us  [swapped_with_each(): lax.ppermute(sent, axis, [(i, i ^ step) for i in range(size)])]
  transfers between devices with their start and end apart: 6 -> 12, of which waited for: 4 -> 5; matrix products, arithmetic and copies ran while one was open for 22% -> 23% of each run, Pallas kernels for 0% -> 0%
where the time goes in v1:
time: 179 us
  waiting for transfers between devices  79.9 us (45%)
  starting transfers between devices  30.2 us (17%)
  matrix products  21 us (12%)
  local copies, waits for them, and re-layouts  20.8 us (12%)
  between operations  14.5 us (8%)
  other arithmetic  12.2 us (7%)
    all_gather x1, waiting for transfers between devices, per_device(): lax.all_gather(face_local, 'dom', axis=0, tiled=True)  65.8 us
    unnamed x24, local copies, waits for them, and re-layouts  14.8 us
    dot_general x2, matrix products, one_sided(): jnp.einsum('rcj,rij->rci', column_side, blocks, preferred_element_type=jn...  10.4 us
    ppermute x7, starting transfers between devices, swapped_with_each(): lax.ppermute(sent, axis, [(i, i ^ step) for i in range(size)])  9.34 us
    all_to_all x1, waiting for transfers between devices, per_device(): lax.all_to_all(inner_packed, 'dom', split_axis=0, concat_axis=0, tiled=True)  8.92 us
    all_to_all x1, starting transfers between devices, per_device(): lax.all_to_all(inner_ids, 'dom', split_axis=0, concat_axis=0, tiled=True)  8.42 us
    all_to_all x1, starting transfers between devices, per_device(): lax.all_to_all(inner_packed, 'dom', split_axis=0, concat_axis=0, tiled=True)  6.93 us
    dot_general x3, matrix products, coarse_terms(): jnp.einsum('rci,rdi->rcd', row_side, products, preferred_element_type=jnp...  6.62 us
  transfers between devices with their start and end apart: 12, of which 5 were waited for; matrix products, arithmetic and copies ran while one was open for 23% of the time, Pallas kernels for 0%

profile of v1, /device:TPU:1, one launch (start us, length us, event | category | flops | bytes accessed | tf_op | source)
XLA Modules:
  0.0 178.6 jit_solution(18259577969441913857)
XLA Ops:
  7.2 0.7 fusion.25
  7.9 0.8 select_reduce_fusion.1
  8.8 0.7 multiply_add_fusion
  9.5 0.1 select_reduce_fusion
  9.6 0.7 sub.86
  10.2 8.4 %all-to-all-start.1 = ((s32[16,1,3]{2,1,0:T(1,128)}), s32[16,1,3]{2,1,0:T(1,128)S(1)}, u32[]{:S(2)}, u32[]{:S(2)}) async-start(s32[16,1,3]{2,1,0:T(1,128)} %bitcast.23), calls=%async_computation.1 | async-start | bytes 16384 | tf_op jit(solution)/shard_map/all_to_all | solution.py:148
  18.9 0.1 mul.177
  19.2 0.1 mul.179
  19.5 0.1 copy.75
  19.6 4.3 %fusion.15 = f32[16,48,48]{2,1,0:T(8,128)S(1)} fusion(bf16[16,384,384]{2,1,0:T(8,128)(2,1)} %param.12, f32[48,384]{1,0:T(8,128)S(1)} %copy.75, f32[16,384]{1,0:T(8,128)} %param.15), kind=kOutput, calls=%fused_computation.26 | convolution fusion | flops 256278528 | bytes 4964352 | tf_op jit(solution)/shard_map/rci,rdi->rcd/dot_general | solution.py:70
  23.9 0.8 reshape.416
  24.9 0.2 select_reduce_fusion.3
  25.1 0.4 fusion.34
  25.5 1.0 broadcast_multiply_fusion.1
  26.5 0.4 fusion.26
  26.9 1.9 %broadcast_multiply_fusion = bf16[32,48,6,4,4,4]{1,0,5,4,3,2:T(8,128)(2,1)S(1)} fusion(f32[48,6,4,4,4]{0,4,3,2,1:T(4,128)S(1)} %broadcast_multiply_fusion.2, f32[32,6,4,4,4]{0,4,3,2,1:T(4,128)S(1)} %bitcast.78), kind=kLoop, calls=%fused_computation.15 | loop fusion | flops 1179648 | bytes 1302528 | tf_op jit(solution)/shard_map/mul | solution.py:40
  29.0 0.6 reverse_select_fusion.5
  29.6 0.7 reverse_select_fusion.4
  30.4 0.8 fusion.1
  31.1 2.6 %fusion.12 = bf16[16,48,384]{2,1,0:T(8,128)(2,1)} fusion(bf16[16,384,384]{2,1,0:T(8,128)(2,1)S(1)} %bitcast.70, bf16[16,48,384]{1,0,2:T(8,128)(2,1)S(1)} %bitcast.67), kind=kOutput, calls=%fused_computation.24 | convolution fusion | flops 226787328 | bytes 5898240 | tf_op jit(solution)/shard_map/rcj,rij->rci/dot_general | solution.py:64
  33.8 1.0 reverse_select_fusion.2
  34.8 1.2 copy.95
  36.0 1.4 convolution_convert_fusion.1
  37.4 1.3 reverse_select_fusion.1
  38.7 1.1 fusion
  39.9 2.2 %copy.96 = bf16[3,8,48,384]{3,2,1,0:T(8,128)(2,1)} copy(bf16[3,8,48,384]{3,1,2,0:T(8,128)(2,1)} %bitcast.73) | data formatting | bytes 1769472
  42.1 5.4 %all-to-all-start = ((bf16[8,3,48,384]{3,2,1,0:T(8,128)(2,1)}), bf16[8,3,48,384]{3,2,1,0:T(8,128)(2,1)}, u32[]{:S(2)}, u32[]{:S(2)}) async-start(bf16[8,3,48,384]{3,2,1,0:T(8,128)(2,1)} %bitcast.72), calls=%async_computation | async-start | bytes 1769472 | tf_op jit(solution)/shard_map/all_to_all | solution.py:138
  47.6 7.7 %fusion.9 = bf16[32,48,384]{2,1,0:T(8,128)(2,1)S(1)} fusion(bf16[32,384,384]{2,1,0:T(8,128)(2,1)} %param.13, bf16[32,48,384]{1,0,2:T(8,128)(2,1)S(1)} %bitcast.65), kind=kOutput, calls=%fused_computation.23 | convolution fusion | flops 453574656 | bytes 11796480 | tf_op jit(solution)/shard_map/rcj,rij->rci/dot_general | solution.py:64
  55.3 0.3 copy.97
  55.6 0.7 convolution_convert_fusion
  56.3 1.4 copy.98
  57.7 3.1 %all-to-all-done = bf16[8,3,48,384]{3,2,1,0:T(8,128)(2,1)} async-done(((bf16[8,3,48,384]{3,2,1,0:T(8,128)(2,1)}), bf16[8,3,48,384]{3,2,1,0:T(8,128)(2,1)}, u32[]{:S(2)}, u32[]{:S(2)}) %all-to-all-start) | async-done | bytes 884768 | tf_op jit(solution)/shard_map/all_to_all | solution.py:138
  60.9 6.9 %all-to-all-start.2 = ((bf16[16,3,48,384]{3,2,1,0:T(8,128)(2,1)}), bf16[16,3,48,384]{3,2,1,0:T(8,128)(2,1)S(1)}, u32[]{:S(2)}, u32[]{:S(2)}) async-start(bf16[16,3,48,384]{3,2,1,0:T(8,128)(2,1)} %bitcast.38), calls=%async_computation.2 | async-start | bytes 3538944 | tf_op jit(solution)/shard_map/all_to_all | solution.py:147
  67.9 1.3 collective-permute-start
  69.2 0.3 collective-permute-start.1
  69.5 1.4 collective-permute-start.2
  71.0 0.4 collective-permute-start.3
  71.4 2.9 %collective-permute-start.4 = (s32[1,3]{1,0:T(1,128)S(1)}, s32[1,3]{1,0:T(1,128)S(1)}, u32[]{:S(2)}, u32[]{:S(2)}) collective-permute-start(s32[1,3]{1,0:T(1,128)S(1)} %get-tuple-element.4), channel_id=1, source_target_pairs={{0,80},{16,64},{32,112},{48,96},{64,16},{80,0},{96,48},{112,32},{1... | collective-permute-start | bytes 44 | tf_op jit(solution)/shard_map/ppermute | solution.py:25
  74.2 0.1 copy.76
  74.3 1.0 collective-permute-start.5
  75.3 0.1 copy.77
  75.4 2.0 %collective-permute-start.6 = (s32[1,3]{1,0:T(1,128)S(1)}, s32[1,3]{1,0:T(1,128)S(1)}, u32[]{:S(2)}, u32[]{:S(2)}) collective-permute-start(s32[1,3]{1,0:T(1,128)S(1)} %get-tuple-element.2), channel_id=1, source_target_pairs={{0,112},{16,96},{32,80},{48,64},{64,48},{80,32},{96,16},{112,0},{1... | collective-permute-start | bytes 44 | tf_op jit(solution)/shard_map/ppermute | solution.py:25
  77.5 0.1 copy.78
  77.5 0.1 copy.79
  77.8 0.6 collective-permute-done.5
  78.4 0.1 copy.82
  78.5 1.4 collective-permute-done.6
  80.0 0.1 stack.49
  80.2 0.6 gather_fusion
  80.9 0.2 fusion.30
  81.1 0.5 broadcast.941
  81.6 0.7 reduce.3
  82.4 0.2 fusion.24
  82.6 1.6 fusion.16
  84.2 0.3 reshape_reshape.8
  84.5 0.3 fusion.23
  84.8 8.9 %all-to-all-done.2 = bf16[16,3,48,384]{3,2,1,0:T(8,128)(2,1)S(1)} async-done(((bf16[16,3,48,384]{3,2,1,0:T(8,128)(2,1)}), bf16[16,3,48,384]{3,2,1,0:T(8,128)(2,1)S(1)}, u32[]{:S(2)}, u32[]{:S(2)}) %all-to-all-start.2) | async-done | bytes 1769504 | tf_op jit(solution)/shard_map/all_to_all | solution.py:147
  93.7 0.7 fusion.4
  94.5 0.5 reshape_reshape.9
  95.0 0.3 convolution_add_fusion
  95.4 0.9 reshape.423
  96.3 65.8 %all-gather.5.cloned.1.call-done = f32[256,6912]{1,0:T(8,128)} async-done(((f32[16,6912]{1,0:T(8,128)}), f32[256,6912]{1,0:T(8,128)}) %all-gather.5.cloned.1.call-update) | async-done | bytes 7077904 | tf_op jit(solution)/shard_map/all_gather | solution.py:158
  162.1 3.2 %copy.109 = f32[256,2304]{1,0:T(8,128)} copy(f32[256,2304]{1,0:T(8,128)} %all-gather.3.cloned.1.call-done) | data formatting | bytes 4718592
  165.3 6.4 %copy.110 = f32[256,6912]{1,0:T(8,128)} copy(f32[256,6912]{1,0:T(8,128)} %all-gather.5.cloned.1.call-done) | data formatting | bytes 14155776
  (61 shorter events, 1.7 us)
Async XLA Ops:
  10.2 31.9 %all-to-all-start.1 = ((s32[16,1,3]{2,1,0:T(1,128)}), s32[16,1,3]{2,1,0:T(1,128)S(1)}, u32[]{:S(2)}, u32[]{:S(2)}) async-start(s32[16,1,3]{2,1,0:T(1,128)} %bitcast.23), calls=%async_computation.1 | async-start | bytes 16384 | tf_op jit(solution)/shard_map/all_to_all | solution.py:148
  18.7 77.6 %all-gather.3.cloned.1.call-start = ((), (), s32[]{:S(2)}) async-start(), calls=%async_computation.3 | async-start | bytes 2506752 | tf_op jit(solution)/shard_map/all_gather | solution.py:157
  19.6 5.2 %copy-start.1 = (s32[16,1]{0,1:T(1,128)S(1)}, s32[16,1]{0,1:T(1,128)}, u32[]{:S(2)}) copy-start(s32[16,1]{0,1:T(1,128)} %param.21) | copy-start | bytes 196
  19.6 5.5 %copy-start = (f32[16,384]{1,0:T(8,128)S(1)}, f32[16,384]{1,0:T(8,128)}, u32[]{:S(2)}) copy-start(f32[16,384]{1,0:T(8,128)} %param.15) | copy-start | bytes 73732
  19.6 5.5 %copy-start.2 = (s32[16]{0:T(128)S(1)}, s32[16]{0:T(128)}, u32[]{:S(2)}) copy-start(s32[16]{0:T(128)} %param.17) | copy-start | bytes 196
  23.9 2.6 %copy-start.5 = (s32[16]{0:T(128)S(1)}, s32[16]{0:T(128)}, u32[]{:S(2)}) copy-start(s32[16]{0:T(128)} %param.19) | copy-start | bytes 196
  23.9 2.6 %copy-start.3 = (s32[32]{0:T(128)S(1)}, s32[32]{0:T(128)}, u32[]{:S(2)}) copy-start(s32[32]{0:T(128)} %param.16) | copy-start | bytes 388
  26.5 2.4 %copy-start.6 = (s32[32]{0:T(128)S(1)}, s32[32]{0:T(128)}, u32[]{:S(2)}) copy-start(s32[32]{0:T(128)} %param.18) | copy-start | bytes 388
  26.5 2.4 %copy-start.4 = (s32[16]{0:T(128)S(1)}, s32[16]{0:T(128)}, u32[]{:S(2)}) copy-start(s32[16]{0:T(128)} %param.23) | copy-start | bytes 196
  26.9 4.2 %slice-start = ((s8[4718592]{0:T(1024)(128)(4,1)}), s8[4194304]{0:T(1024)(128)(4,1)S(1)}, s32[]{:S(2)}) async-start(s8[4718592]{0:T(1024)(128)(4,1)} %bitcast.69), calls=%async_computation.5 | async-start | bytes 8388608
  29.0 2.1 %slice-start.1 = ((s8[4718592]{0:T(1024)(128)(4,1)}), s8[524288]{0:T(1024)(128)(4,1)S(1)}, s32[]{:S(2)}) async-start(s8[4718592]{0:T(1024)(128)(4,1)} %bitcast.69), calls=%async_computation.6 | async-start | bytes 1048576
  42.1 18.8 %all-to-all-start = ((bf16[8,3,48,384]{3,2,1,0:T(8,128)(2,1)}), bf16[8,3,48,384]{3,2,1,0:T(8,128)(2,1)}, u32[]{:S(2)}, u32[]{:S(2)}) async-start(bf16[8,3,48,384]{3,2,1,0:T(8,128)(2,1)} %bitcast.72), calls=%async_computation | async-start | bytes 1769472 | tf_op jit(solution)/shard_map/all_to_all | solution.py:138
  60.9 32.9 %all-to-all-start.2 = ((bf16[16,3,48,384]{3,2,1,0:T(8,128)(2,1)}), bf16[16,3,48,384]{3,2,1,0:T(8,128)(2,1)S(1)}, u32[]{:S(2)}, u32[]{:S(2)}) async-start(bf16[16,3,48,384]{3,2,1,0:T(8,128)(2,1)} %bitcast.38), calls=%async_computation.2 | async-start | bytes 3538944 | tf_op jit(solution)/shard_map/all_to_all | solution.py:147
  67.8 94.3 %all-gather.5.cloned.1.call-start = ((), (), s32[]{:S(2)}) async-start(), calls=%async_computation.4 | async-start | bytes 7520256 | tf_op jit(solution)/shard_map/all_gather | solution.py:158
  67.9 6.4 %collective-permute-start = (s32[1,3]{1,0:T(1,128)S(1)}, s32[1,3]{1,0:T(1,128)S(1)}, u32[]{:S(2)}, u32[]{:S(2)}) collective-permute-start(s32[1,3]{1,0:T(1,128)S(1)} %get-tuple-element.8), channel_id=1, source_target_pairs={{0,16},{16,0},{32,48},{48,32},{64,80},{80,64},{96,112},{112,96},{1... | collective-permute-start | bytes 44 | tf_op jit(solution)/shard_map/ppermute | solution.py:25
  69.2 6.2 %collective-permute-start.1 = (s32[1,3]{1,0:T(1,128)S(1)}, s32[1,3]{1,0:T(1,128)S(1)}, u32[]{:S(2)}, u32[]{:S(2)}) collective-permute-start(s32[1,3]{1,0:T(1,128)S(1)} %get-tuple-element.7), channel_id=1, source_target_pairs={{0,32},{16,48},{32,0},{48,16},{64,96},{80,112},{96,64},{112,80},{1... | collective-permute-start | bytes 44 | tf_op jit(solution)/shard_map/ppermute | solution.py:25
  69.5 8.0 %collective-permute-start.2 = (s32[1,3]{1,0:T(1,128)S(1)}, s32[1,3]{1,0:T(1,128)S(1)}, u32[]{:S(2)}, u32[]{:S(2)}) collective-permute-start(s32[1,3]{1,0:T(1,128)S(1)} %get-tuple-element.6), channel_id=1, source_target_pairs={{0,48},{16,32},{32,16},{48,0},{64,112},{80,96},{96,80},{112,64},{1... | collective-permute-start | bytes 44 | tf_op jit(solution)/shard_map/ppermute | solution.py:25
  71.0 6.7 %collective-permute-start.3 = (s32[1,3]{1,0:T(1,128)S(1)}, s32[1,3]{1,0:T(1,128)S(1)}, u32[]{:S(2)}, u32[]{:S(2)}) collective-permute-start(s32[1,3]{1,0:T(1,128)S(1)} %get-tuple-element.5), channel_id=1, source_target_pairs={{0,64},{16,80},{32,96},{48,112},{64,0},{80,16},{96,32},{112,48},{1... | collective-permute-start | bytes 44 | tf_op jit(solution)/shard_map/ppermute | solution.py:25
  71.4 6.4 %collective-permute-start.4 = (s32[1,3]{1,0:T(1,128)S(1)}, s32[1,3]{1,0:T(1,128)S(1)}, u32[]{:S(2)}, u32[]{:S(2)}) collective-permute-start(s32[1,3]{1,0:T(1,128)S(1)} %get-tuple-element.4), channel_id=1, source_target_pairs={{0,80},{16,64},{32,112},{48,96},{64,16},{80,0},{96,48},{112,32},{1... | collective-permute-start | bytes 44 | tf_op jit(solution)/shard_map/ppermute | solution.py:25
  74.3 4.1 %collective-permute-start.5 = (s32[1,3]{1,0:T(1,128)S(1)}, s32[1,3]{1,0:T(1,128)S(1)}, u32[]{:S(2)}, u32[]{:S(2)}) collective-permute-start(s32[1,3]{1,0:T(1,128)S(1)} %get-tuple-element.3), channel_id=1, source_target_pairs={{0,96},{16,112},{32,64},{48,80},{64,32},{80,48},{96,0},{112,16},{1... | collective-permute-start | bytes 44 | tf_op jit(solution)/shard_map/ppermute | solution.py:25
  75.4 4.5 %collective-permute-start.6 = (s32[1,3]{1,0:T(1,128)S(1)}, s32[1,3]{1,0:T(1,128)S(1)}, u32[]{:S(2)}, u32[]{:S(2)}) collective-permute-start(s32[1,3]{1,0:T(1,128)S(1)} %get-tuple-element.2), channel_id=1, source_target_pairs={{0,112},{16,96},{32,80},{48,64},{64,48},{80,32},{96,16},{112,0},{1... | collective-permute-start | bytes 44 | tf_op jit(solution)/shard_map/ppermute | solution.py:25
Sparse Core Ops, SparseCore 0:
  24.9 46.2 all-gather.2
  96.4 65.6 all-gather.4
